TPU v7x, 32 devices: a whole 2x2x4 slice. The times are simulated.
32 devices in a mesh: mem: 8 (over z, core), dom: 4 (over y, x).
Axes of the slice: x: 2, y: 2, z: 4, core: 2. Of those that a mesh axis runs over, the one named last changes fastest.
Arguments:
- prior_ensemble: float32 [64, 4, 512, 512], P('mem', None, 'dom'), may hold values from -6 to 6
- spreading_factor: float32 [4], replicated, may hold values from 0.05 to 0.24
- tendency_matrix: float32 [4, 4], replicated, may hold values from -0.6 to 0.6
- measured_data: float32 [4, 4096], P('dom', 'mem'), may hold values from -6 to 6
- inverse_error: float32 [4, 4096], P('dom', 'mem'), may hold values from 0.1 to 1
- assigned_subregion: int32 [4, 4096, 1], P('dom', 'mem'), may hold values from 0 to 31; in each aligned block of 512 rows (0 to 511, 512 to 1023, ..., all dimensions but the last counted through in order) at most 32 rows name the same one
- measured_entry: int32 [4, 4096], P('dom', 'mem'), may hold values from 0 to 8191
- taper_index: int32 [4, 4096], P('dom', 'mem'), may hold values from 0 to 63
- taper_factors: float32 [64], replicated, may hold values from 0.2 to 1
Outputs:
- analysis: float32 [64, 4, 512, 512], P('mem', None, 'dom')
Inputs may be any that keep to these rules, and one draw needn't show every extreme that they name: `assigned_subregion`: in the rows of one device no patch is named by more than 32 rows, a bound that some block reaches.
All inputs are finite; a program needn't handle non-finite values.
Results may differ from a plain program's by a relative error of at most 0.0003.
Values sent between devices are 32-bit elements; how exact they have to be, the bound alone decides.
A program may use at most 128 MiB of HBM per device.

v0:
```python
import jax
import jax.numpy as jnp
from jax import lax
from jax.sharding import PartitionSpec as P

PATCH = 2048
NS_ITERS = 5
HIGH = lax.Precision.HIGHEST


def padded(block, sides, width):
    for axis, dim in sides:
        count = lax.axis_size(axis)
        forward = [(i, i + 1) for i in range(count - 1)]
        backward = [(target, source) for source, target in forward]
        low = lax.ppermute(
            lax.slice_in_dim(block, block.shape[dim] - width, None, axis=dim), axis, forward
        )
        high = lax.ppermute(lax.slice_in_dim(block, 0, width, axis=dim), axis, backward)
        block = jnp.concatenate([low, block, high], axis=dim)
    return block


def laplacian_update(haloed_ensemble, ensemble, spreading_factor, tendency_matrix):
    subdomain_lines = ensemble.shape[2]
    beside = jnp.pad(ensemble, ((0, 0), (0, 0), (0, 0), (1, 1)))
    laplace = (
        haloed_ensemble[:, :, 2:]
        + haloed_ensemble[:, :, :subdomain_lines]
        + beside[:, :, :, 2:]
        + beside[:, :, :, :-2]
        - 4.0 * ensemble
    )
    mixing = jnp.einsum("vw,kwxy->kvxy", tendency_matrix, ensemble, precision=HIGH)
    return ensemble + spreading_factor[None, :, None, None] * laplace + mixing


def transforms(gram, drive, member_count):
    identity_m = jnp.eye(member_count, dtype=jnp.float32)
    system = (member_count - 1.0) * identity_m + gram
    norm_value = jnp.sqrt(jnp.sum(system * system, axis=(-2, -1)))
    iterate = system / norm_value[..., None, None]
    inverse = jnp.broadcast_to(identity_m, system.shape)
    for sweep_no in range(NS_ITERS):
        middle = 1.5 * identity_m - 0.5 * jnp.einsum(
            "...ij,...jk->...ik", inverse, iterate, precision=HIGH
        )
        iterate = jnp.einsum("...ij,...jk->...ik", iterate, middle, precision=HIGH)
        inverse = jnp.einsum("...ij,...jk->...ik", middle, inverse, precision=HIGH)
    root = inverse / jnp.sqrt(norm_value)[..., None, None]
    inner = jnp.einsum("...ij,...j->...i", root, drive, precision=HIGH)
    offset = jnp.einsum("...ij,...j->...i", root, inner, precision=HIGH)
    return offset[..., :, None] + jnp.sqrt(member_count - 1.0) * root


def slot_ranks(patch_ids, patch_count):
    onehot = (patch_ids[..., None] == jnp.arange(patch_count, dtype=jnp.int32)).astype(jnp.int32)
    before = jnp.cumsum(onehot, axis=-2) - onehot
    return jnp.sum(before * onehot, axis=-1)


def shards(
    prior_ensemble,
    spreading_factor,
    tendency_matrix,
    measured_data,
    inverse_error,
    assigned_subregion,
    measured_entry,
    taper_index,
    taper_factors,
):
    ensemble_share, prognostic_number, subdomain_lines, eastward_span = prior_ensemble.shape
    groups = lax.axis_size("mem")
    members = ensemble_share * groups
    cells_dev = subdomain_lines * eastward_span // groups
    per_device = cells_dev // PATCH
    per_tile = per_device * groups
    haloed_ensemble = padded(prior_ensemble, (("dom", 2),), 1)
    advanced_ensemble = laplacian_update(
        haloed_ensemble, prior_ensemble, spreading_factor, tendency_matrix
    )
    moved = lax.all_to_all(
        advanced_ensemble.reshape(ensemble_share, prognostic_number, groups, cells_dev),
        "mem",
        split_axis=2,
        concat_axis=0,
        tiled=True,
    )
    ensemble = moved.reshape(members, prognostic_number, cells_dev)
    patch_ids = assigned_subregion.reshape(-1)
    obs_rows = patch_ids.shape[0]
    capacity = 2 * obs_rows // per_tile
    table_levels = taper_factors.shape[0]
    picks = (
        taper_index.reshape(-1)[:, None] == jnp.arange(table_levels, dtype=jnp.int32)[None, :]
    ).astype(jnp.float32)
    weight = inverse_error.reshape(-1) * jnp.dot(picks, taper_factors, precision=HIGH)
    values = measured_data.reshape(-1)
    columns = measured_entry.reshape(-1).astype(jnp.float32)
    target = patch_ids * capacity + slot_ranks(patch_ids, per_tile)

    def place_rows(field):
        return (
            jnp.zeros((per_tile * capacity,), jnp.float32)
            .at[target]
            .set(field)
            .reshape(groups, per_device * capacity)
        )

    received = (
        lax.all_to_all(place_rows(values), "mem", split_axis=0, concat_axis=0, tiled=True),
        lax.all_to_all(place_rows(weight), "mem", split_axis=0, concat_axis=0, tiled=True),
        lax.all_to_all(place_rows(columns), "mem", split_axis=0, concat_axis=0, tiled=True),
    )

    def arrange(field):
        return (
            field.reshape(groups, per_device, capacity)
            .transpose(1, 0, 2)
            .reshape(per_device, groups * capacity)
        )

    slot_value = arrange(received[0])
    slot_weight = arrange(received[1])
    slot_column = arrange(received[2])
    centre = jnp.mean(ensemble, axis=0)
    deviation = ensemble - centre[None]
    column_ids = slot_column.astype(jnp.int32)
    flat_index = (
        column_ids // PATCH * cells_dev
        + jnp.arange(per_device, dtype=jnp.int32)[:, None] * PATCH
        + column_ids % PATCH
    )
    flat_index = flat_index.reshape(-1)
    flat_dev = deviation.reshape(members, prognostic_number * cells_dev)
    obs_dev = jnp.take(flat_dev, flat_index, axis=1).reshape(members, per_device, -1)
    innovation = slot_value - jnp.take(centre.reshape(-1), flat_index).reshape(per_device, -1)
    weighted = obs_dev * slot_weight[None]
    gram = jnp.einsum("kps,jps->pkj", weighted, obs_dev, precision=HIGH)
    drive = jnp.einsum("kps,ps->pk", weighted, innovation, precision=HIGH)
    coeffs = transforms(gram, drive, members)
    dev_blocks = deviation.reshape(members, prognostic_number, per_device, PATCH)
    mixed = jnp.einsum("pjk,jvpt->kvpt", coeffs, dev_blocks, precision=HIGH)
    analysed = centre.reshape(1, prognostic_number, per_device, PATCH) + mixed
    outgoing = analysed.reshape(groups, ensemble_share, prognostic_number, cells_dev)
    returned = lax.all_to_all(outgoing, "mem", split_axis=0, concat_axis=3, tiled=True)
    return returned.reshape(ensemble_share, prognostic_number, subdomain_lines, eastward_span)


def solution(mesh):
    in_specs = (
        P("mem", None, "dom", None),
        P(),
        P(),
        P("dom", "mem"),
        P("dom", "mem"),
        P("dom", "mem", None),
        P("dom", "mem"),
        P("dom", "mem"),
        P(),
    )
    out_specs = P("mem", None, "dom", None)
    return jax.shard_map(shards, mesh=mesh, in_specs=in_specs, out_specs=out_specs, check_vma=False)
```

profile of v0, /device:TPU:0, one launch (start us, length us, event | category | flops | bytes accessed | tf_op | source)
XLA Modules:
  0.0 609.6 jit_solution(14362782641976846216)
XLA Ops:
  0.0 0.7 fusion.39
  0.7 1.2 reduce-window.6
  2.1 0.8 fusion.33
  2.9 0.7 compare_select_fusion.1
  3.6 0.7 convert_element_type.53
  4.3 3.0 scatter_custom_fusion
  7.3 6.4 %all-to-all-start.1 = ((f32[8,1,128]{2,1,0:T(1,128)}), f32[8,1,128]{2,1,0:T(1,128)S(1)}, u32[]{:S(2)}, u32[]{:S(2)}) async-start(f32[8,1,128]{2,1,0:T(1,128)} %bitcast.14), calls=%async_computation.1 | async-start | bytes 8192 | tf_op jit(solution)/shard_map/all_to_all | solution.py:114
  13.6 1.3 fusion.63
  15.0 1.3 collective-permute-start
  16.3 4.7 collective-permute-start.1
  21.0 25.0 %fusion.8 = f32[8,128,512,4]{2,3,1,0:T(4,128)} fusion(f32[8,4,128,512]{3,2,1,0:T(8,128)} %param.9, f32[4,4]{1,0:T(4,128)S(1)} %copy-done), kind=kOutput, calls=%fused_computation.19 | convolution fusion | flops 100663296 | bytes 16777280 | tf_op jit(solution)/shard_map/vw,kwxy->kvxy/dot_general | solution.py:34
  46.0 3.2 scatter_custom_fusion.2
  49.1 5.1 all-to-all-start.3
  54.3 0.3 fusion.18
  54.6 3.0 scatter_custom_fusion.1
  57.6 2.2 all-to-all-done.3
  59.8 3.2 all-to-all-start.2
  63.1 22.8 %fusion.5 = f32[8,4,128,512]{3,2,1,0:T(8,128)} fusion(f32[8,4,128,512]{3,2,1,0:T(8,128)} %param.9, f32[8,4,1,512]{3,2,1,0:T(1,128)S(1)} %collective-permute-done.1, f32[8,4,1,512]{3,2,1,0:T(1,128)S(1)} %collective-permute-done, f32[8,128,512,4]{2,3,1,0:T(4,128)} %fusion.8, f32[4]{0:T(128)S(1)} %copy-done.3), kind=kLoop, calls=%fused_computation.12 | loop fusion | flops 20971520 | bytes 25296912 | tf_op jit(solution)/shard_map/add | solution.py:35
  85.9 9.4 %reshape.273 = f32[8,4,8,8192]{3,2,1,0:T(8,128)} reshape(f32[8,4,128,512]{3,2,1,0:T(8,128)} %fusion.5) | data formatting | bytes 16777216 | tf_op jit(solution)/shard_map/reshape | solution.py:84
  95.3 12.0 %copy.84 = f32[8,4,8,8192]{3,1,0,2:T(4,128)} copy(f32[8,4,8,8192]{3,2,1,0:T(8,128)} %reshape.273) | data formatting | bytes 16777216 | tf_op jit(solution)/shard_map/reshape | solution.py:84
  107.3 5.3 all-to-all-start
  113.0 0.5 broadcast.335
  113.5 0.7 reduce.14
  114.3 0.7 reduce.13
  115.2 181.3 %all-to-all-done = f32[8,4,8,8192]{3,1,0,2:T(4,128)} async-done(((f32[8,4,8,8192]{3,1,0,2:T(4,128)}), f32[8,4,8,8192]{3,1,0,2:T(4,128)}, u32[]{:S(2)}, u32[]{:S(2)}) %all-to-all-start) | async-done | bytes 8388640 | tf_op jit(solution)/shard_map/all_to_all | solution.py:83
  296.5 4.2 bitcast_reduce_fusion
  300.7 6.2 %gather_fusion.1 = f32[1024]{0:T(1024)S(1)} fusion(f32[32768]{0:T(1024)S(1)} %bitcast.131, s32[1024]{0:T(1024)S(1)} %broadcast_clamp_fusion), kind=kCustom, calls=%fused_computation.1 | custom fusion | bytes 12288 | tf_op jit(solution)/shard_map/jit(_take)/gather | solution.py:138
  306.9 8.1 %copy.111 = f32[8,8,4,8192]{3,1,2,0:T(8,128)S(1)} copy(f32[8,8,4,8192]{3,2,1,0:T(4,128)} %bitcast.56) | data formatting | bytes 16777216
  315.1 4.0 broadcast_subtract_fusion
  319.1 12.2 %copy.90 = f32[64,32768]{0,1:T(8,128)} copy(f32[64,32768]{1,0:T(8,128)} %broadcast_subtract_fusion) | data formatting | bytes 16777216 | tf_op jit(solution)/shard_map/sub | solution.py:128
  331.3 8.6 %gather_fusion = f32[1024,64]{1,0:T(8,128)S(1)} fusion(f32[64,32768]{0,1:T(8,128)} %copy.90, s32[1024]{0:T(1024)S(1)} %broadcast_clamp_fusion), kind=kCustom, calls=%fused_computation | custom fusion | bytes 528384 | tf_op jit(solution)/shard_map/jit(_take)/gather | solution.py:137
  340.2 0.5 multiply_reduce_fusion
  340.7 0.3 fusion.15
  341.0 0.3 fusion.43
  341.6 0.3 fusion.14
  342.4 0.3 fusion.13
  344.0 0.3 convolution_bitcast_fusion.1
  344.3 0.3 fusion.11
  344.9 0.3 convolution_bitcast_fusion
  345.2 0.3 fusion.70
  345.5 12.1 %reshape.334 = f32[64,4,4,2048]{3,2,1,0:T(4,128)} reshape(f32[8,8,4,1,8192]{4,2,1,0,3:T(4,128)} %bitcast.4) | data formatting | bytes 16777216 | tf_op jit(solution)/shard_map/reshape | solution.py:90
  357.6 20.7 %bitcast_add_fusion = f32[64,4,4,2048]{3,0,1,2:T(8,128)} fusion(f32[64,4,4,2048]{3,2,1,0:T(4,128)} %reshape.334, f32[4,4,2048]{2,0,1:T(4,128)S(1)} %bitcast.136, f32[4,64,64]{2,1,0:T(8,128)S(1)} %convolution_divide_fusion, f32[4,64]{1,0:T(4,128)S(1)} %bitcast.140), kind=kOutput, calls=%fused_computation.16 | convolution fusion | flops 1614839808 | bytes 16974848 | tf_op jit(solution)/shard_map/pjk,jvpt->kvpt/dot_general | solution.py:144
  378.3 12.2 %copy.95 = f32[64,4,4,2048]{3,2,0,1:T(4,128)} copy(f32[64,4,4,2048]{3,0,1,2:T(8,128)} %bitcast_add_fusion) | data formatting | bytes 16777216 | tf_op jit(solution)/shard_map/add | solution.py:145
  390.5 10.9 %reshape.282 = f32[8,8,4,8192]{3,1,0,2:T(8,128)} reshape(f32[64,4,4,2048]{3,2,0,1:T(4,128)} %copy.95) | data formatting | bytes 16777216 | tf_op jit(solution)/shard_map/reshape | solution.py:146
  401.3 3.9 copy.96
  405.3 186.6 %all_to_all.57 = f32[8,8,4,8192]{3,1,2,0:T(8,128)S(1)} all-to-all(f32[8,8,4,8192]{3,1,2,0:T(8,128)S(1)} %copy.96), channel_id=1, replica_groups=mesh['mem'=8,'dom'=4] {'mem'}, dimensions={0} | all-to-all | bytes 16777216 | tf_op jit(solution)/shard_map/all_to_all | solution.py:147
  591.9 8.1 %copy.97 = f32[1,8,4,8,8192]{4,3,2,1,0:T(8,128)} copy(f32[1,8,4,8,8192]{4,1,2,3,0:T(8,128)S(1)} %bitcast.134) | data formatting | bytes 16777216 | tf_op jit(solution)/shard_map/all_to_all | solution.py:147
  600.0 9.4 %reshape.283 = f32[8,4,128,512]{3,2,1,0:T(8,128)} reshape(f32[1,8,4,8,8192]{4,3,2,1,0:T(8,128)} %copy.97) | data formatting | bytes 16777216 | tf_op jit(solution)/shard_map/reshape | solution.py:148
  (54 shorter events, 3.7 us)
Async XLA Ops:
  0.0 21.0 %copy-start = (f32[4,4]{1,0:T(4,128)S(1)}, f32[4,4]{1,0:T(4,128)}, u32[]{:S(2)}) copy-start(f32[4,4]{1,0:T(4,128)} %param.11) | copy-start | bytes 196
  7.3 41.9 %all-to-all-start.1 = ((f32[8,1,128]{2,1,0:T(1,128)}), f32[8,1,128]{2,1,0:T(1,128)S(1)}, u32[]{:S(2)}, u32[]{:S(2)}) async-start(f32[8,1,128]{2,1,0:T(1,128)} %bitcast.14), calls=%async_computation.1 | async-start | bytes 8192 | tf_op jit(solution)/shard_map/all_to_all | solution.py:114
  15.0 48.1 %collective-permute-start = (f32[8,4,1,512]{3,2,1,0:T(1,128)S(1)}, f32[8,4,1,512]{3,2,1,0:T(1,128)S(1)}, u32[]{:S(2)}, u32[]{:S(2)}) collective-permute-start(f32[8,4,1,512]{3,2,1,0:T(1,128)S(1)} %get-tuple-element.7), channel_id=1, source_target_pairs={{1,0},{2,1},{3,2},{5,4},{6,5},{7,6},{9,8},{10,9},{11,10},{13,12},{... | collective-permute-start | bytes 196616 | tf_op jit(solution)/shard_map/ppermute | solution.py:19
  16.3 38.0 %copy-start.4 = (s32[1,512]{1,0:T(1,128)S(1)}, s32[1,512]{1,0:T(1,128)}, u32[]{:S(2)}) copy-start(s32[1,512]{1,0:T(1,128)} %param.16) | copy-start | bytes 6148
  16.3 38.0 %copy-start.5 = (f32[64]{0:T(128)S(1)}, f32[64]{0:T(128)}, u32[]{:S(2)}) copy-start(f32[64]{0:T(128)} %param.17) | copy-start | bytes 772
  16.3 38.3 %copy-start.2 = (f32[1,512]{1,0:T(1,128)S(1)}, f32[1,512]{1,0:T(1,128)}, u32[]{:S(2)}) copy-start(f32[1,512]{1,0:T(1,128)} %param.13) | copy-start | bytes 6148
  16.3 46.8 %copy-start.3 = (f32[4]{0:T(128)S(1)}, f32[4]{0:T(128)}, u32[]{:S(2)}) copy-start(f32[4]{0:T(128)} %param.10) | copy-start | bytes 52
  16.3 46.8 %collective-permute-start.1 = (f32[8,4,1,512]{3,2,1,0:T(1,128)S(1)}, f32[8,4,1,512]{3,2,1,0:T(1,128)S(1)}, u32[]{:S(2)}, u32[]{:S(2)}) collective-permute-start(f32[8,4,1,512]{3,2,1,0:T(1,128)S(1)} %get-tuple-element.8), channel_id=1, source_target_pairs={{0,1},{1,2},{2,3},{4,5},{5,6},{6,7},{8,9},{9,10},{10,11},{12,13},{... | collective-permute-start | bytes 196616 | tf_op jit(solution)/shard_map/ppermute | solution.py:16
  49.1 10.7 %all-to-all-start.3 = ((f32[8,1,128]{2,1,0:T(1,128)}), f32[8,1,128]{2,1,0:T(1,128)S(1)}, u32[]{:S(2)}, u32[]{:S(2)}) async-start(f32[8,1,128]{2,1,0:T(1,128)} %bitcast.26), calls=%async_computation.3 | async-start | bytes 8192 | tf_op jit(solution)/shard_map/all_to_all | solution.py:112
  59.8 47.5 %all-to-all-start.2 = ((f32[8,1,128]{2,1,0:T(1,128)}), f32[8,1,128]{2,1,0:T(1,128)S(1)}, u32[]{:S(2)}, u32[]{:S(2)}) async-start(f32[8,1,128]{2,1,0:T(1,128)} %bitcast.23), calls=%async_computation.2 | async-start | bytes 8192 | tf_op jit(solution)/shard_map/all_to_all | solution.py:113
  107.3 189.2 %all-to-all-start = ((f32[8,4,8,8192]{3,1,0,2:T(4,128)}), f32[8,4,8,8192]{3,1,0,2:T(4,128)}, u32[]{:S(2)}, u32[]{:S(2)}) async-start(f32[8,4,8,8192]{3,1,0,2:T(4,128)} %copy.84), calls=%async_computation | async-start | bytes 16777216 | tf_op jit(solution)/shard_map/all_to_all | solution.py:83
  591.9 17.4 %copy-start.1 = (f32[4,4]{1,0:T(4,128)S(1)}, f32[4,4]{1,0:T(4,128)}, u32[]{:S(2)}) copy-start(f32[4,4]{1,0:T(4,128)} %param.11) | copy-start | bytes 196
where the time goes:
time: 621 us; the launch traced here: 610 us
  blocking collectives  187 us (30%)
  waiting for transfers between devices  183 us (29%)
  local copies, waits for them, and re-layouts  125 us (20%)
  matrix products  51.1 us (8%)
  other arithmetic  36.7 us (6%)
  starting transfers between devices  25.9 us (4%)
    all_to_all x1, blocking collectives, shards(): lax.all_to_all(outgoing, 'mem', split_axis=0, concat_axis=3, tiled=True)  187 us
    all_to_all x1, waiting for transfers between devices, shards(): lax.all_to_all(advanced_ensemble.reshape(ensemble_share, prognostic_numbe...  181 us
    dot_general x1, matrix products, laplacian_update(): jnp.einsum('vw,kwxy->kvxy', tendency_matrix, ensemble, precision=HIGH)  25 us
    add x1, other arithmetic, laplacian_update(): return ensemble + spreading_factor[None, :, None, None] * laplace + mixing  22.8 us
    reshape x2, local copies, waits for them, and re-layouts, shards(): advanced_ensemble.reshape(ensemble_share, prognostic_number, groups, cell...  21.3 us
    dot_general x1, matrix products, shards(): mixed = jnp.einsum('pjk,jvpt->kvpt', coeffs, dev_blocks, precision=HIGH)  20.7 us
    reshape x2, local copies, waits for them, and re-layouts, shards(): analysed.reshape(groups, ensemble_share, prognostic_number, cells_dev)  14.8 us
  transfers between devices with their start and end apart: 6, of which 2 were waited for; matrix products, arithmetic and copies ran while one was open for 13% of the time, Pallas kernels for 0%

commit v1 on v0

--- a/solution.py
+++ b/solution.py
@@ -144,7 +144,10 @@
     mixed = jnp.einsum("pjk,jvpt->kvpt", coeffs, dev_blocks, precision=HIGH)
     analysed = centre.reshape(1, prognostic_number, per_device, PATCH) + mixed
     outgoing = analysed.reshape(groups, ensemble_share, prognostic_number, cells_dev)
-    returned = lax.all_to_all(outgoing, "mem", split_axis=0, concat_axis=3, tiled=True)
+    returned = jnp.concatenate(
+        lax.all_to_all(jnp.stack(jnp.split(outgoing, lax.axis_size("mem"), axis=0)), "mem", 0, 0),
+        axis=3,
+    )
     return returned.reshape(ensemble_share, prognostic_number, subdomain_lines, eastward_span)
 
 

time: 621 us -> 649 us (1.045)
  local copies, waits for them, and re-layouts: 125 us -> 153 us
    another operation x1 -> x11, local copies, waits for them, and re-layouts: 0.01 us -> 34.4 us  [the longest x9 25.1 us: shards(): jnp.stack(jnp.split(outgoing, lax.axis_size('mem'), axis=0))]
    split x0 -> x9, local copies, waits for them, and re-layouts: none -> 20.7 us  [shards(): jnp.split(outgoing, lax.axis_size('mem'), axis=0)]
    reshape x3 -> x1, local copies, waits for them, and re-layouts: 24.2 us -> 8.08 us  [shards(): jnp.concatenate(lax.all_to_all(jnp.stack(jnp.split(outgoing, lax.axis_siz...]
    add x1 -> x0, local copies, waits for them, and re-layouts: 12.2 us -> none  [shards(): analysed = centre.reshape(1, prognostic_number, per_device, PATCH) + mixed]
    unnamed x16 -> x35, local copies, waits for them, and re-layouts: 8.26 us -> 18 us
    all_to_all x1 -> x0, local copies, waits for them, and re-layouts: 8.08 us -> none  [shards(): lax.all_to_all(outgoing, 'mem', split_axis=0, concat_axis=3, tiled=True)]
  transfers between devices with their start and end apart: 6 -> 6, of which waited for: 2 -> 2; matrix products, arithmetic and copies ran while one was open for 13% -> 12% of each run, Pallas kernels for 0% -> 0%
where the time goes in v1:
time: 649 us; the launch traced here: 638 us
  blocking collectives  188 us (29%)
  waiting for transfers between devices  183 us (28%)
  local copies, waits for them, and re-layouts  153 us (24%)
  matrix products  49.4 us (8%)
  other arithmetic  36.7 us (6%)
  starting transfers between devices  26.1 us (4%)
    all_to_all x1, blocking collectives, shards(): lax.all_to_all(jnp.stack(jnp.split(outgoing, lax.axis_size('mem'), axis=0...  188 us
    all_to_all x1, waiting for transfers between devices, shards(): lax.all_to_all(advanced_ensemble.reshape(ensemble_share, prognostic_numbe...  181 us
    another operation x9, local copies, waits for them, and re-layouts, shards(): jnp.stack(jnp.split(outgoing, lax.axis_size('mem'), axis=0))  25.1 us
    dot_general x1, matrix products, laplacian_update(): jnp.einsum('vw,kwxy->kvxy', tendency_matrix, ensemble, precision=HIGH)  25 us
    add x1, other arithmetic, laplacian_update(): return ensemble + spreading_factor[None, :, None, None] * laplace + mixing  22.8 us
    reshape x2, local copies, waits for them, and re-layouts, shards(): advanced_ensemble.reshape(ensemble_share, prognostic_number, groups, cell...  21.3 us
    split x9, local copies, waits for them, and re-layouts, shards(): jnp.split(outgoing, lax.axis_size('mem'), axis=0)  20.7 us
    dot_general x1, matrix products, shards(): mixed = jnp.einsum('pjk,jvpt->kvpt', coeffs, dev_blocks, precision=HIGH)  19 us
  transfers between devices with their start and end apart: 6, of which 2 were waited for; matrix products, arithmetic and copies ran while one was open for 12% of the time, Pallas kernels for 0%

profile of v1, /device:TPU:0, one launch (start us, length us, event | category | flops | bytes accessed | tf_op | source)
XLA Modules:
  0.0 637.6 jit_solution(12470243655348502270)
XLA Ops:
  0.7 1.2 reduce-window.6
  4.3 3.0 scatter_custom_fusion
  7.3 6.4 all-to-all-start.1
  13.6 1.3 fusion.64
  15.0 1.3 collective-permute-start
  16.3 4.7 collective-permute-start.1
  21.0 25.0 %fusion.8 = f32[8,128,512,4]{2,3,1,0:T(4,128)} fusion(f32[8,4,128,512]{3,2,1,0:T(8,128)} %param.9, f32[4,4]{1,0:T(4,128)S(1)} %copy-done), kind=kOutput, calls=%fused_computation.19 | convolution fusion | flops 100663296 | bytes 16777280 | tf_op jit(solution)/shard_map/vw,kwxy->kvxy/dot_general | solution.py:34
  46.0 3.2 scatter_custom_fusion.2
  49.1 5.1 all-to-all-start.3
  54.6 3.0 scatter_custom_fusion.1
  57.6 2.2 all-to-all-done.3
  59.8 3.2 all-to-all-start.2
  63.1 22.8 %fusion.5 = f32[8,4,128,512]{3,2,1,0:T(8,128)} fusion(f32[8,4,128,512]{3,2,1,0:T(8,128)} %param.9, f32[8,4,1,512]{3,2,1,0:T(1,128)S(1)} %collective-permute-done.1, f32[8,4,1,512]{3,2,1,0:T(1,128)S(1)} %collective-permute-done, f32[8,128,512,4]{2,3,1,0:T(4,128)} %fusion.8, f32[4]{0:T(128)S(1)} %copy-done.9), kind=kLoop, calls=%fused_computation.12 | loop fusion | flops 20971520 | bytes 25296912 | tf_op jit(solution)/shard_map/add | solution.py:35
  85.9 9.4 %reshape.286 = f32[8,4,8,8192]{3,2,1,0:T(8,128)} reshape(f32[8,4,128,512]{3,2,1,0:T(8,128)} %fusion.5) | data formatting | bytes 16777216 | tf_op jit(solution)/shard_map/reshape | solution.py:84
  95.3 12.0 %copy.104 = f32[8,4,8,8192]{3,1,0,2:T(4,128)} copy(f32[8,4,8,8192]{3,2,1,0:T(8,128)} %reshape.286) | data formatting | bytes 16777216 | tf_op jit(solution)/shard_map/reshape | solution.py:84
  107.3 5.5 all-to-all-start
  115.4 181.3 %all-to-all-done = f32[8,4,8,8192]{3,1,0,2:T(4,128)} async-done(((f32[8,4,8,8192]{3,1,0,2:T(4,128)}), f32[8,4,8,8192]{3,1,0,2:T(4,128)}, u32[]{:S(2)}, u32[]{:S(2)}) %all-to-all-start) | async-done | bytes 8388640 | tf_op jit(solution)/shard_map/all_to_all | solution.py:83
  296.7 4.2 bitcast_reduce_fusion
  300.9 6.2 gather_fusion.1
  307.1 8.1 %copy.137 = f32[8,8,4,8192]{3,1,2,0:T(8,128)S(1)} copy(f32[8,8,4,8192]{3,2,1,0:T(4,128)} %bitcast.54) | data formatting | bytes 16777216
  315.2 4.0 broadcast_subtract_fusion
  319.3 12.2 %copy.110 = f32[64,32768]{0,1:T(8,128)} copy(f32[64,32768]{1,0:T(8,128)} %broadcast_subtract_fusion) | data formatting | bytes 16777216 | tf_op jit(solution)/shard_map/sub | solution.py:128
  331.5 8.6 %gather_fusion = f32[1024,64]{1,0:T(8,128)S(1)} fusion(f32[64,32768]{0,1:T(8,128)} %copy.110, s32[1024]{0:T(1024)S(1)} %broadcast_clamp_fusion), kind=kCustom, calls=%fused_computation | custom fusion | bytes 528384 | tf_op jit(solution)/shard_map/jit(_take)/gather | solution.py:137
  345.7 11.9 %reshape.346 = f32[64,4,4,2048]{3,2,1,0:T(4,128)} reshape(f32[8,8,4,1,8192]{4,2,1,0,3:T(4,128)} %bitcast.4) | data formatting | bytes 16777216 | tf_op jit(solution)/shard_map/reshape | solution.py:90
  357.6 19.0 %bitcast_add_fusion = f32[64,4,4,2048]{3,0,1,2:T(8,128)S(1)} fusion(f32[64,4,4,2048]{3,2,1,0:T(4,128)} %reshape.346, f32[4,4,2048]{2,0,1:T(4,128)S(1)} %bitcast.148, f32[4,64,64]{2,1,0:T(8,128)S(1)} %convolution_divide_fusion, f32[4,64]{1,0:T(4,128)S(1)} %bitcast.152), kind=kOutput, calls=%fused_computation.16 | convolution fusion | flops 1614839808 | bytes 16974848 | tf_op jit(solution)/shard_map/pjk,jvpt->kvpt/dot_general | solution.py:144
  376.6 2.5 fusion.63
  379.0 1.6 copy.115
  380.7 2.9 stack.27
  383.6 2.3 constant_dynamic-update-slice_fusion.7
  385.9 2.9 copy.116
  388.7 2.9 stack.28
  391.7 2.9 copy.117
  394.6 3.0 stack.29
  397.5 2.9 copy.118
  400.4 2.9 stack.30
  403.3 2.9 copy.119
  406.2 2.9 stack.31
  409.1 1.7 copy.120
  410.8 3.0 stack.32
  413.8 1.7 copy.121
  415.5 3.0 stack.33
  418.6 1.7 copy.122
  420.2 3.3 stack.34
  423.5 1.0 constant_dynamic-update-slice_fusion.6
  425.6 2.3 constant_dynamic-update-slice_fusion.4
  432.0 187.6 %all_to_all.47 = f32[8,1,8,4,8192]{4,2,3,1,0:T(8,128)S(1)} all-to-all(f32[8,1,8,4,8192]{4,2,3,1,0:T(8,128)} %constant_dynamic-update-slice_fusion), channel_id=1, replica_groups=mesh['mem'=8,'dom'=4] {'mem'}, dimensions={0} | all-to-all | bytes 16777216 | tf_op jit(solution)/shard_map/all_to_all | solution.py:148
  619.7 8.1 %copy.123 = f32[1,8,4,8,8192]{4,3,2,1,0:T(8,128)} copy(f32[1,8,4,8,8192]{4,1,2,0,3:T(8,128)S(1)} %bitcast.146) | data formatting | bytes 16777216 | tf_op jit(solution)/shard_map/reshape | solution.py:147
  627.8 9.4 %reshape_reshape.3 = f32[8,4,128,512]{3,2,1,0:T(8,128)} reshape(f32[1,8,4,8,8192]{4,3,2,1,0:T(8,128)} %copy.123) | data formatting | bytes 16777216 | tf_op jit(solution)/shard_map/reshape;reshape | solution.py:151
  (88 shorter events, 16.8 us)
Async XLA Ops:
  0.0 21.0 %copy-start = (f32[4,4]{1,0:T(4,128)S(1)}, f32[4,4]{1,0:T(4,128)}, u32[]{:S(2)}) copy-start(f32[4,4]{1,0:T(4,128)} %param.11) | copy-start | bytes 196
  7.3 41.9 %all-to-all-start.1 = ((f32[8,1,128]{2,1,0:T(1,128)}), f32[8,1,128]{2,1,0:T(1,128)S(1)}, u32[]{:S(2)}, u32[]{:S(2)}) async-start(f32[8,1,128]{2,1,0:T(1,128)} %bitcast.14), calls=%async_computation.1 | async-start | bytes 8192 | tf_op jit(solution)/shard_map/all_to_all | solution.py:114
  15.0 48.1 %collective-permute-start = (f32[8,4,1,512]{3,2,1,0:T(1,128)S(1)}, f32[8,4,1,512]{3,2,1,0:T(1,128)S(1)}, u32[]{:S(2)}, u32[]{:S(2)}) collective-permute-start(f32[8,4,1,512]{3,2,1,0:T(1,128)S(1)} %get-tuple-element.15), channel_id=1, source_target_pairs={{1,0},{2,1},{3,2},{5,4},{6,5},{7,6},{9,8},{10,9},{11,10},{13,12},{... | collective-permute-start | bytes 196616 | tf_op jit(solution)/shard_map/ppermute | solution.py:19
  16.3 38.0 %copy-start.10 = (s32[1,512]{1,0:T(1,128)S(1)}, s32[1,512]{1,0:T(1,128)}, u32[]{:S(2)}) copy-start(s32[1,512]{1,0:T(1,128)} %param.16) | copy-start | bytes 6148
  16.3 38.0 %copy-start.11 = (f32[64]{0:T(128)S(1)}, f32[64]{0:T(128)}, u32[]{:S(2)}) copy-start(f32[64]{0:T(128)} %param.17) | copy-start | bytes 772
  16.3 38.3 %copy-start.8 = (f32[1,512]{1,0:T(1,128)S(1)}, f32[1,512]{1,0:T(1,128)}, u32[]{:S(2)}) copy-start(f32[1,512]{1,0:T(1,128)} %param.13) | copy-start | bytes 6148
  16.3 46.8 %copy-start.9 = (f32[4]{0:T(128)S(1)}, f32[4]{0:T(128)}, u32[]{:S(2)}) copy-start(f32[4]{0:T(128)} %param.10) | copy-start | bytes 52
  16.3 46.8 %collective-permute-start.1 = (f32[8,4,1,512]{3,2,1,0:T(1,128)S(1)}, f32[8,4,1,512]{3,2,1,0:T(1,128)S(1)}, u32[]{:S(2)}, u32[]{:S(2)}) collective-permute-start(f32[8,4,1,512]{3,2,1,0:T(1,128)S(1)} %get-tuple-element.16), channel_id=1, source_target_pairs={{0,1},{1,2},{2,3},{4,5},{5,6},{6,7},{8,9},{9,10},{10,11},{12,13},{... | collective-permute-start | bytes 196616 | tf_op jit(solution)/shard_map/ppermute | solution.py:16
  49.1 10.7 %all-to-all-start.3 = ((f32[8,1,128]{2,1,0:T(1,128)}), f32[8,1,128]{2,1,0:T(1,128)S(1)}, u32[]{:S(2)}, u32[]{:S(2)}) async-start(f32[8,1,128]{2,1,0:T(1,128)} %bitcast.26), calls=%async_computation.3 | async-start | bytes 8192 | tf_op jit(solution)/shard_map/all_to_all | solution.py:112
  59.8 47.5 %all-to-all-start.2 = ((f32[8,1,128]{2,1,0:T(1,128)}), f32[8,1,128]{2,1,0:T(1,128)S(1)}, u32[]{:S(2)}, u32[]{:S(2)}) async-start(f32[8,1,128]{2,1,0:T(1,128)} %bitcast.23), calls=%async_computation.2 | async-start | bytes 8192 | tf_op jit(solution)/shard_map/all_to_all | solution.py:113
  107.3 189.4 %all-to-all-start = ((f32[8,4,8,8192]{3,1,0,2:T(4,128)}), f32[8,4,8,8192]{3,1,0,2:T(4,128)}, u32[]{:S(2)}, u32[]{:S(2)}) async-start(f32[8,4,8,8192]{3,1,0,2:T(4,128)} %copy.104), calls=%async_computation | async-start | bytes 16777216 | tf_op jit(solution)/shard_map/all_to_all | solution.py:83
  410.8 12.7 %copy-start.2 = (f32[1,1,8,4,8192]{4,2,3,1,0:T(8,128)S(1)}, f32[1,1,8,4,8192]{4,2,3,1,0:T(8,128)}, u32[]{:S(2)}) copy-start(f32[1,1,8,4,8192]{4,2,3,1,0:T(8,128)} %stack.28) | copy-start | bytes 3145732
  415.5 9.0 %copy-start.3 = (f32[1,1,8,4,8192]{4,2,3,1,0:T(8,128)S(1)}, f32[1,1,8,4,8192]{4,2,3,1,0:T(8,128)}, u32[]{:S(2)}) copy-start(f32[1,1,8,4,8192]{4,2,3,1,0:T(8,128)} %stack.29) | copy-start | bytes 3145732
  420.2 7.6 %copy-start.4 = (f32[1,1,8,4,8192]{4,2,3,1,0:T(8,128)S(1)}, f32[1,1,8,4,8192]{4,2,3,1,0:T(8,128)}, u32[]{:S(2)}) copy-start(f32[1,1,8,4,8192]{4,2,3,1,0:T(8,128)} %stack.31) | copy-start | bytes 3145732
  423.5 5.4 copy-start.5
  423.5 6.4 %copy-start.6 = (f32[1,1,8,4,8192]{4,2,3,1,0:T(8,128)S(1)}, f32[1,1,8,4,8192]{4,2,3,1,0:T(8,128)}, u32[]{:S(2)}) copy-start(f32[1,1,8,4,8192]{4,2,3,1,0:T(8,128)} %stack.33) | copy-start | bytes 3145732
  423.5 7.5 %copy-start.7 = (f32[1,1,8,4,8192]{4,2,3,1,0:T(8,128)S(1)}, f32[1,1,8,4,8192]{4,2,3,1,0:T(8,128)}, u32[]{:S(2)}) copy-start(f32[1,1,8,4,8192]{4,2,3,1,0:T(8,128)} %stack.34) | copy-start | bytes 3145732
  619.7 17.4 %copy-start.1 = (f32[4,4]{1,0:T(4,128)S(1)}, f32[4,4]{1,0:T(4,128)}, u32[]{:S(2)}) copy-start(f32[4,4]{1,0:T(4,128)} %param.11) | copy-start | bytes 196
